TPU v7x, 256 devices: a whole 4x4x8 slice. The times are simulated.
256 devices in a mesh: sens: 8 (over z_lo, core), pts: 32 (over y, z_hi, x).
Axes of the slice: x: 4, y: 4, z: 8 (z_hi: 2, z_lo: 4; z = z_hi * 4 + z_lo), core: 2. Of those that a mesh axis runs over, the one named last changes fastest.
Arguments:
- kernel: float32 [64, 2048, 384], P('sens', 'pts'), may hold values from -0.0068359375 to 0.0068359375
- vectors: float32 [8, 2048, 384], P(None, 'pts'), may hold values from -6 to 6
- noise_scale: float32 [64], P('sens'), may hold values from 0.5 to 2
- sensor_group: int32 [64], P('sens'), may hold values from 0 to 3
- correlation: float32 [4, 384, 384], replicated, may hold values from -0.3125 to 0.3125
- stiffness: float32 [2048], P('pts'), may hold values from 0.2 to 1
- couplings: float32 [4, 2048], P(None, 'pts'), may hold values from 0.05 to 0.5
- neighbors: int32 [4, 2048], P(None, 'pts'), may hold values from 0 to 2047, as said below
Outputs:
- hessian_action: float32 [8, 2048, 384], P('sens', 'pts')
Inputs may be any that keep to these rules, and one draw needn't show every extreme that they name: `neighbors`: points are numbered row by row on a grid of rows of 16 points; every neighbor of point p lies in p's grid row or in one of the two rows beside it.
All inputs are finite; a program needn't handle non-finite values.
Results may differ from a plain program's by a relative error of at most 0.0001.
Values sent between devices are 32-bit elements; how exact they have to be, the bound alone decides.
A program may use at most 64 MiB of HBM per device.

v0:
```python
import math
import jax
import jax.numpy as jnp
from jax import lax
from jax.sharding import PartitionSpec as P

COLS = 16
HIGHEST = lax.Precision.HIGHEST


def padded_2(block, sides, width):
    for axis, dim in sides:
        count = lax.axis_size(axis)
        forward = [(i, i + 1) for i in range(count - 1)]
        backward = [(target, source) for source, target in forward]
        low = lax.ppermute(
            lax.slice_in_dim(block, block.shape[dim] - width, None, axis=dim), axis, forward
        )
        high = lax.ppermute(lax.slice_in_dim(block, 0, width, axis=dim), axis, backward)
        block = jnp.concatenate([low, block, high], axis=dim)
    return block


def tables(length):
    span = 2 * length
    steps = lax.iota(jnp.int32, length)
    phase = steps[:, None] * steps[None, :] % span
    angle = phase.astype(jnp.float32) * (2.0 * math.pi / span)
    cosine = jnp.cos(angle)
    sine = jnp.sin(angle)
    nyquist = jnp.where(steps % 2 == 0, 1.0, -1.0).astype(jnp.float32)
    first_col = steps == 0
    second = jnp.where(first_col[None, :], nyquist[:, None], -sine)
    forward = jnp.concatenate([cosine, second], axis=1)
    weight = jnp.where(first_col, 1.0, 2.0).astype(jnp.float32)
    back_first = cosine * weight[:, None]
    back_second = jnp.where(first_col[:, None], nyquist[None, :], -2.0 * sine)
    inverse = jnp.concatenate([back_first, back_second], axis=0) / span
    return (forward, inverse)


def spectral(left, right, form, half):
    left_x, left_y = (left[..., :half], left[..., half:])
    right_x, right_y = (right[..., :half], right[..., half:])
    prod_xx = jnp.einsum(form, left_x, right_x, precision=HIGHEST)
    prod_yy = jnp.einsum(form, left_y, right_y, precision=HIGHEST)
    prod_xy = jnp.einsum(form, left_x, right_y, precision=HIGHEST)
    prod_yx = jnp.einsum(form, left_y, right_x, precision=HIGHEST)
    keep = (lax.iota(jnp.int32, half) > 0).astype(jnp.float32)
    real_part = prod_xx - keep * prod_yy
    imag_part = keep * (prod_xy + prod_yx) + (1.0 - keep) * prod_yy
    return jnp.concatenate([real_part, imag_part], axis=-1)


def weight_rows(rows, row_ids, noise_scale, sensor_group, correlation):
    sensors = noise_scale.shape[0]
    groups = correlation.shape[0]
    pick = (row_ids[:, None] % sensors == lax.iota(jnp.int32, sensors)[None, :]).astype(jnp.float32)
    group_table = (sensor_group[:, None] == lax.iota(jnp.int32, groups)[None, :]).astype(
        jnp.float32
    )
    row_scale = jnp.dot(pick, noise_scale, precision=HIGHEST)
    row_group = jnp.dot(pick, group_table, precision=HIGHEST)
    mixed = jnp.einsum("rt,but->rbu", rows, correlation, precision=HIGHEST)
    extra = jnp.einsum("rbu,rb->ru", mixed, row_group, precision=HIGHEST)
    return row_scale[:, None] * (rows + extra)


def local(kernel, vectors, noise_scale, sensor_group, correlation, stiffness, couplings, neighbors):
    sensors, points, length = kernel.shape
    count = vectors.shape[0]
    forward, inverse = tables(length)
    kern_hat = jnp.einsum("spt,tf->spf", kernel, forward, precision=HIGHEST)
    vec_hat = jnp.einsum("kpt,tf->kpf", vectors, forward, precision=HIGHEST)
    pred_hat = spectral(vec_hat, kern_hat, "kpf,spf->ksf", length)
    partial_value = jnp.einsum("ksf,ft->kst", pred_hat, inverse, precision=HIGHEST)
    flat = partial_value.reshape(count * sensors, length)
    predicted = lax.psum(flat, "pts")
    row_ids = lax.iota(jnp.int32, count * sensors)
    weighted = weight_rows(predicted, row_ids, noise_scale, sensor_group, correlation)
    residual = weighted.reshape(count, sensors, length)
    res_hat = jnp.einsum("kst,tf->ksf", residual, forward, precision=HIGHEST)
    columns = lax.iota(jnp.int32, 2 * length)
    flip = jnp.where(columns > length, -1.0, 1.0).astype(jnp.float32)
    conj_hat = kern_hat * flip
    grad_hat = spectral(res_hat, conj_hat, "ksf,spf->kpf", length)
    own_count = count // lax.axis_size("sens")
    data_term = lax.psum_scatter(
        jnp.einsum("kpf,ft->kpt", grad_hat, inverse, precision=HIGHEST),
        "sens",
        scatter_dimension=0,
        tiled=True,
    )
    own_vectors = lax.dynamic_slice_in_dim(
        vectors, lax.axis_index("sens") * own_count, own_count, 0
    )
    padded = padded_2(own_vectors, (("pts", 1),), COLS)
    local_index = neighbors - lax.axis_index("pts") * points + COLS
    gathered = jnp.take(padded, local_index, axis=1)
    prior_term = stiffness[None, :, None] * own_vectors
    prior_term = prior_term + jnp.sum(
        couplings[None, :, :, None] * (own_vectors[:, None] - gathered), axis=1
    )
    return data_term + prior_term


def solution(mesh):
    in_specs = (
        P("sens", "pts", None),
        P(None, "pts", None),
        P("sens"),
        P("sens"),
        P(),
        P("pts"),
        P(None, "pts"),
        P(None, "pts"),
    )
    out_specs = P("sens", "pts", None)
    return jax.shard_map(local, mesh=mesh, in_specs=in_specs, out_specs=out_specs, check_vma=False)
```

profile of v0, /device:TPU:12, one launch (start us, length us, event | category | flops | bytes accessed | tf_op | source)
XLA Modules:
  0.0 537.6 jit_solution(15899717636893823764)
XLA Ops:
  6.5 0.0 copy-start
  6.6 2.2 fusion.13
  8.8 3.3 multiply_select_fusion
  12.2 0.0 copy-done.14
  12.2 2.7 broadcast_multiply_fusion
  14.9 1.7 fusion.47
  16.7 2.8 copy.15
  19.4 3.8 convolution_bitcast_fusion
  23.2 1.4 fusion.49
  24.6 2.8 copy.16
  27.4 2.8 copy.23
  30.2 5.8 %fusion.51 = f32[384,8,8]{2,1,0:T(8,128)} fusion(f32[8,64,384]{1,0,2:T(8,128)} %copy.15, f32[8,64,384]{1,0,2:T(8,128)} %copy.16), kind=kOutput, calls=%fused_computation.86 | convolution fusion | flops 18874368 | bytes 1671168 | tf_op jit(solution)/shard_map/kpf,spf->ksf/dot_general | solution.py:46
  36.0 0.0 copy-done.7
  36.1 4.0 fusion.52
  40.1 2.9 copy.22
  43.0 6.4 %subtract_bitcast_fusion.1 = f32[8,8,384]{0,1,2:T(8,128)} fusion(f32[384,8,8]{2,1,0:T(8,128)} %fusion.51, f32[8,64,384]{1,0,2:T(8,128)} %copy.22, f32[8,64,384]{1,0,2:T(8,128)} %copy.23, f32[384]{0:T(512)S(1)} %fusion.38), kind=kOutput, calls=%fused_computation.7 | convolution fusion | flops 18923520 | bytes 1771008 | tf_op jit(solution)/shard_map/kpf,spf->ksf/dot_general | solution.py:45
  49.3 0.0 copy-done.4
  49.4 4.4 add_bitcast_fusion.1
  53.8 2.5 copy.18
  56.2 2.5 copy.17
  58.7 2.3 broadcast_multiply_fusion.1
  61.0 0.8 copy-done.11
  61.8 2.6 convolution_bitcast_fusion.2
  64.4 0.0 all-reduce.2.cloned.1.call-update
  64.4 0.4 reduce-scatter.2.cloned.1.call-start
  64.9 0.6 and_select_fusion
  65.5 2.8 copy.19
  68.3 2.8 copy.27
  71.1 0.0 copy-done.20
  71.1 1.5 fusion.28
  72.5 0.8 convolution_bitcast_fusion.3
  73.4 370.9 %all-reduce.2.cloned.1.call-done = f32[64,384]{1,0:T(8,128)} async-done(((f32[64,384]{1,0:T(8,128)}), f32[64,384]{1,0:T(8,128)}) %all-reduce.2.cloned.1.call-update) | async-done | bytes 98320 | tf_op jit(solution)/shard_map/psum | solution.py:78
  444.3 0.0 copy-done
  444.3 3.4 fusion.24
  447.7 0.0 copy-done.16
  447.7 1.2 fusion.15
  448.9 0.8 fusion.5
  449.8 1.7 copy.29
  451.5 1.7 copy.28
  453.2 5.4 fusion.53
  458.5 0.0 copy-done.6
  458.5 0.0 copy-done.9
  458.5 3.5 fusion.54
  462.1 3.6 subtract_bitcast_fusion
  465.7 4.2 add_bitcast_fusion
  469.9 0.2 pad_maximum_fusion
  470.1 0.8 copy-done.12
  470.9 0.2 copy-done.13
  471.1 6.6 %fusion = f32[8,64,384]{2,1,0:T(8,128)} fusion(f32[8,64,768]{1,0,2:T(8,128)S(1)} %pad_maximum_fusion, f32[384,384]{1,0:T(8,128)S(1)} %copy-done.13, f32[384,384]{1,0:T(8,128)S(1)} %copy-done.12), kind=kOutput, calls=%fused_computation.2 | convolution fusion | flops 1812529152 | bytes 3538944 | tf_op jit(solution)/shard_map/kpf,ft->kpt/dot_general | solution.py:89
  477.7 0.0 reduce-scatter.2.cloned.1.call-update
  477.8 0.8 constant_dynamic-slice_fusion.1
  478.5 1.9 collective-permute-start
  480.4 3.9 collective-permute-start.1
  484.4 0.1 reshape.106
  484.5 0.9 constant_dynamic-slice_fusion.2
  485.4 0.9 fusion.75
  486.3 0.0 collective-permute-done
  486.3 0.7 collective-permute-done.1
  487.1 0.0 copy-start.17
  487.1 0.0 copy-start.19
  487.1 1.0 gather_fusion
  488.1 0.1 multiply_reduce_fusion
  488.2 40.6 %reduce-scatter.2.cloned.1.call-done = f32[1,64,384]{2,1,0:T(8,128)} async-done(((f32[8,64,384]{2,1,0:T(8,128)}), f32[1,64,384]{2,1,0:T(8,128)}) %reduce-scatter.2.cloned.1.call-update) | async-done | bytes 98320 | tf_op jit(solution)/shard_map/reduce_scatter | solution.py:88
  528.9 1.7 fusion.20
  (41 shorter events, 0.1 us)
Async XLA Ops:
  6.5 437.8 %copy-start = (f32[4,384,384]{2,1,0:T(8,128)S(1)}, f32[4,384,384]{2,1,0:T(8,128)}, u32[]{:S(2)}) copy-start(f32[4,384,384]{2,1,0:T(8,128)} %param.12) | copy-start | bytes 7077892
  6.5 437.8 %all-reduce.2.cloned.1.call-start = ((), (), s32[]{:S(2)}) async-start(), calls=%async_computation.1 | async-start | bytes 196608 | tf_op jit(solution)/shard_map/psum | solution.py:78
  6.5 5.6 %copy-start.14 = (f32[8,64,384]{2,1,0:T(8,128)S(1)}, f32[8,64,384]{2,1,0:T(8,128)}, u32[]{:S(2)}) copy-start(f32[8,64,384]{2,1,0:T(8,128)} %param.8) | copy-start | bytes 2359300
  30.2 5.9 %copy-start.7 = (f32[8,64,384]{1,0,2:T(8,128)S(1)}, f32[8,64,384]{1,0,2:T(8,128)}, u32[]{:S(2)}) copy-start(f32[8,64,384]{1,0,2:T(8,128)} %copy.15) | copy-start | bytes 2359300
  30.2 5.9 %copy-start.8 = (f32[8,64,384]{1,0,2:T(8,128)S(1)}, f32[8,64,384]{1,0,2:T(8,128)}, u32[]{:S(2)}) copy-start(f32[8,64,384]{1,0,2:T(8,128)} %copy.23) | copy-start | bytes 2359300
  43.0 6.4 %copy-start.3 = (f32[8,64,384]{1,0,2:T(8,128)S(1)}, f32[8,64,384]{1,0,2:T(8,128)}, u32[]{:S(2)}) copy-start(f32[8,64,384]{1,0,2:T(8,128)} %copy.16) | copy-start | bytes 2359300
  43.0 6.4 %copy-start.4 = (f32[384,8,8]{2,1,0:T(8,128)S(1)}, f32[384,8,8]{2,1,0:T(8,128)}, u32[]{:S(2)}) copy-start(f32[384,8,8]{2,1,0:T(8,128)} %fusion.51) | copy-start | bytes 294916
  43.0 6.4 %copy-start.5 = (f32[8,64,384]{1,0,2:T(8,128)S(1)}, f32[8,64,384]{1,0,2:T(8,128)}, u32[]{:S(2)}) copy-start(f32[8,64,384]{1,0,2:T(8,128)} %copy.22) | copy-start | bytes 2359300
  43.0 6.4 %copy-start.10 = (f32[384,8,8]{2,1,0:T(8,128)S(1)}, f32[384,8,8]{2,1,0:T(8,128)}, u32[]{:S(2)}) copy-start(f32[384,8,8]{2,1,0:T(8,128)} %fusion.52) | copy-start | bytes 294916
  61.0 0.8 copy-start.11
  64.4 464.4 %reduce-scatter.2.cloned.1.call-start = ((), (), s32[]{:S(2)}) async-start(), calls=%async_computation.2 | async-start | bytes 884736 | tf_op jit(solution)/shard_map/reduce_scatter | solution.py:88
  68.3 2.8 copy-start.20
  68.3 4.3 copy-start.21
  444.3 3.4 copy-start.16
  444.3 4.6 copy-start.15
  453.1 5.4 copy-start.6
  453.2 5.4 %copy-start.9 = (f32[8,8,384]{0,1,2:T(8,128)S(1)}, f32[8,8,384]{0,1,2:T(8,128)}, u32[]{:S(2)}) copy-start(f32[8,8,384]{0,1,2:T(8,128)} %copy.28) | copy-start | bytes 294916
  458.5 3.5 copy-start.1
  462.1 3.6 copy-start.2
  469.9 1.1 copy-start.12
  469.9 1.2 copy-start.13
  471.1 13.3 %copy-start.18 = (s32[4,64]{1,0:T(4,128)S(1)}, s32[4,64]{1,0:T(4,128)}, u32[]{:S(2)}) copy-start(s32[4,64]{1,0:T(4,128)} %param.15) | copy-start | bytes 3076
  478.5 7.8 %collective-permute-start = (f32[1,16,384]{2,1,0:T(8,128)S(1)}, f32[1,16,384]{2,1,0:T(8,128)S(1)}, u32[]{:S(2)}, u32[]{:S(2)}) collective-permute-start(f32[1,16,384]{2,1,0:T(8,128)S(1)} %get-tuple-element.13), channel_id=1, source_target_pairs={{0,1},{1,2},{2,3},{3,4},{4,5},{5,6},{6,7},{7,8},{8,9},{9,10},{10,1... | collective-permute-start | bytes 73736 | tf_op jit(solution)/shard_map/ppermute | solution.py:16
  480.4 6.6 %collective-permute-start.1 = (f32[1,16,384]{2,1,0:T(8,128)S(1)}, f32[1,16,384]{2,1,0:T(8,128)S(1)}, u32[]{:S(2)}, u32[]{:S(2)}) collective-permute-start(f32[1,16,384]{2,1,0:T(8,128)S(1)} %get-tuple-element.14), channel_id=1, source_target_pairs={{1,0},{2,1},{3,2},{4,3},{5,4},{6,5},{7,6},{8,7},{9,8},{10,9},{11,1... | collective-permute-start | bytes 73736 | tf_op jit(solution)/shard_map/ppermute | solution.py:19
  487.1 1.0 copy-start.17
  487.1 41.8 %copy-start.19 = (f32[64]{0:T(128)S(1)}, f32[64]{0:T(128)}, u32[]{:S(2)}) copy-start(f32[64]{0:T(128)} %param.13) | copy-start | bytes 772
Sparse Core Ops, SparseCore 0:
  64.6 379.6 all-reduce.1
  477.9 50.9 reduce-scatter.1
where the time goes:
time: 541 us; the launch traced here: 538 us
  waiting for transfers between devices  412 us (76%)
  matrix products  60.8 us (11%)
  local copies, waits for them, and re-layouts  33.8 us (6%)
  between operations  13.9 us (3%)
  other arithmetic  10.4 us (2%)
  starting transfers between devices  6.28 us (1%)
    psum x1, waiting for transfers between devices, local(): predicted = lax.psum(flat, 'pts')  371 us
    reduce_scatter x1, waiting for transfers between devices, local(): lax.psum_scatter(jnp.einsum('kpf,ft->kpt', grad_hat, inverse, precision=H...  40.6 us
    slice x5, local copies, waits for them, and re-layouts, spectral(): right_x, right_y = (right[..., :half], right[..., half:])  13 us
    dot_general x2, matrix products, spectral(): prod_yy = jnp.einsum(form, left_y, right_y, precision=HIGHEST)  11.2 us
  transfers between devices with their start and end apart: 4, of which 3 were waited for; matrix products, arithmetic and copies ran while one was open for 2% of the time, Pallas kernels for 0%

commit v1 on v0

--- a/solution.py
+++ b/solution.py
@@ -75,7 +75,7 @@
     pred_hat = spectral(vec_hat, kern_hat, "kpf,spf->ksf", length)
     partial_value = jnp.einsum("ksf,ft->kst", pred_hat, inverse, precision=HIGHEST)
     flat = partial_value.reshape(count * sensors, length)
-    predicted = lax.psum(flat, "pts")
+    predicted = jnp.sum(lax.all_gather(flat, "pts"), 0)
     row_ids = lax.iota(jnp.int32, count * sensors)
     weighted = weight_rows(predicted, row_ids, noise_scale, sensor_group, correlation)
     residual = weighted.reshape(count, sensors, length)

time: 541 us -> 248 us (0.46)
  waiting for transfers between devices: 412 us -> 118 us
    psum x1 -> x0, waiting for transfers between devices: 371 us -> none  [local(): predicted = lax.psum(flat, 'pts')]
    all_gather x0 -> x1, waiting for transfers between devices: none -> 93.9 us  [local(): predicted = jnp.sum(lax.all_gather(flat, 'pts'), 0)]
    reduce_scatter x1, waiting for transfers between devices: 40.6 us -> 22.7 us  [local(): lax.psum_scatter(jnp.einsum('kpf,ft->kpt', grad_hat, inverse, precision=H...]
  transfers between devices with their start and end apart: 4 -> 4, of which waited for: 3 -> 3; matrix products, arithmetic and copies ran while one was open for 2% -> 5% of each run, Pallas kernels for 0% -> 0%
where the time goes in v1:
time: 248 us; the launch traced here: 244 us
  waiting for transfers between devices  118 us (48%)
  matrix products  60.1 us (24%)
  local copies, waits for them, and re-layouts  33.8 us (14%)
  between operations  13.9 us (6%)
  other arithmetic  12.6 us (5%)
  starting transfers between devices  6.28 us (3%)
    all_gather x1, waiting for transfers between devices, local(): predicted = jnp.sum(lax.all_gather(flat, 'pts'), 0)  93.9 us
    reduce_scatter x1, waiting for transfers between devices, local(): lax.psum_scatter(jnp.einsum('kpf,ft->kpt', grad_hat, inverse, precision=H...  22.7 us
    slice x5, local copies, waits for them, and re-layouts, spectral(): right_x, right_y = (right[..., :half], right[..., half:])  13 us
    dot_general x2, matrix products, spectral(): prod_yy = jnp.einsum(form, left_y, right_y, precision=HIGHEST)  11.2 us
    slice x6, local copies, waits for them, and re-layouts, spectral(): left_x, left_y = (left[..., :half], left[..., half:])  10.3 us
    dot_general x2, matrix products, spectral(): prod_xx = jnp.einsum(form, left_x, right_x, precision=HIGHEST)  9.99 us
    dot_general x2, matrix products, spectral(): prod_yx = jnp.einsum(form, left_y, right_x, precision=HIGHEST)  8.56 us
    dot_general x2, matrix products, spectral(): prod_xy = jnp.einsum(form, left_x, right_y, precision=HIGHEST)  7.53 us
  transfers between devices with their start and end apart: 4, of which 3 were waited for; matrix products, arithmetic and copies ran while one was open for 5% of the time, Pallas kernels for 0%

profile of v1, /device:TPU:12, one launch (start us, length us, event | category | flops | bytes accessed | tf_op | source)
XLA Modules:
  0.0 244.4 jit_solution(3560002869766204673)
XLA Ops:
  6.5 0.0 copy-start
  6.5 0.0 all-gather.2.cloned.1.call-start
  6.6 2.2 fusion.13
  8.8 3.3 %multiply_select_fusion = (f32[384,384]{1,0:T(8,128)}, f32[384,384]{1,0:T(8,128)S(1)}) fusion(f32[384]{0:T(512)S(1)} %fusion.36, pred[384]{0:T(512)(128)(4,1)S(1)} %iota_compare_fusion.7), kind=kLoop, calls=%fused_computation.22 | loop fusion | flops 1916928 | bytes 1181568 | tf_op jit(solution)/shard_map/jit(_where)/select_n | solution.py:37
  12.2 0.0 copy-done.15
  12.2 2.7 %broadcast_multiply_fusion = (f32[8,64,768]{2,1,0:T(8,128)S(1)}, f32[8,64,768]{2,1,0:T(8,128)S(1)}) fusion(f32[768]{0:T(1024)S(1)} %fusion.31, f32[8,64,384]{2,1,0:T(8,128)S(1)} %copy-done.15, f32[384,384]{1,0:T(8,128)S(1)} %get-tuple-element.18, f32[384,384]{1,0:T(8,128)S(1)} %fusion.13), kind=kOutput, calls=%fused_computation.16 | convolution fusion | flops 1812627456 | bytes 5114880 | tf_op jit(solution)/shard_map/spt,tf->spf/dot_general | solution.py:73
  14.9 1.8 fusion.47
  16.7 2.8 %copy.15 = f32[8,64,384]{1,0,2:T(8,128)} copy(f32[8,64,384]{2,1,0:T(8,128)} %get-tuple-element.21) | data formatting | bytes 1572864 | tf_op jit(solution)/shard_map/slice | solution.py:44
  19.4 3.8 %convolution_bitcast_fusion = f32[8,64,768]{2,1,0:T(8,128)S(1)} fusion(f32[8,64,384]{2,1,0:T(8,128)} %param.9, f32[384,384]{1,0:T(8,128)S(1)} %get-tuple-element.18, f32[384,384]{1,0:T(8,128)S(1)} %fusion.13), kind=kOutput, calls=%fused_computation.8 | convolution fusion | flops 1812234240 | bytes 3538944 | tf_op jit(solution)/shard_map/kpt,tf->kpf/dot_general | solution.py:74
  23.2 1.4 fusion.49
  24.6 2.8 %copy.16 = f32[8,64,384]{1,0,2:T(8,128)} copy(f32[8,64,384]{2,1,0:T(8,128)} %get-tuple-element.12) | data formatting | bytes 1572864 | tf_op jit(solution)/shard_map/slice | solution.py:43
  27.4 2.8 %copy.23 = f32[8,64,384]{1,0,2:T(8,128)} copy(f32[8,64,384]{2,1,0:T(8,128)} %get-tuple-element.11) | data formatting | bytes 1572864 | tf_op jit(solution)/shard_map/slice | solution.py:43
  30.2 5.8 %fusion.51 = f32[384,8,8]{2,1,0:T(8,128)} fusion(f32[8,64,384]{1,0,2:T(8,128)} %copy.15, f32[8,64,384]{1,0,2:T(8,128)} %copy.16), kind=kOutput, calls=%fused_computation.86 | convolution fusion | flops 18874368 | bytes 1671168 | tf_op jit(solution)/shard_map/kpf,spf->ksf/dot_general | solution.py:46
  36.1 0.0 copy-done.7
  36.1 0.0 copy-done.8
  36.1 4.0 %fusion.52 = f32[384,8,8]{2,1,0:T(8,128)} fusion(f32[8,64,384]{1,0,2:T(8,128)S(1)} %copy-done.7, f32[8,64,384]{1,0,2:T(8,128)S(1)} %copy-done.8), kind=kOutput, calls=%fused_computation.87 | convolution fusion | flops 18874368 | bytes 1671168 | tf_op jit(solution)/shard_map/kpf,spf->ksf/dot_general | solution.py:47
  40.1 2.9 %copy.22 = f32[8,64,384]{1,0,2:T(8,128)} copy(f32[8,64,384]{2,1,0:T(8,128)} %get-tuple-element.22) | data formatting | bytes 1572864 | tf_op jit(solution)/shard_map/slice | solution.py:44
  43.0 6.4 %subtract_bitcast_fusion.1 = f32[8,8,384]{0,1,2:T(8,128)} fusion(f32[384,8,8]{2,1,0:T(8,128)} %fusion.51, f32[8,64,384]{1,0,2:T(8,128)} %copy.22, f32[8,64,384]{1,0,2:T(8,128)} %copy.23, f32[384]{0:T(512)S(1)} %fusion.38), kind=kOutput, calls=%fused_computation.7 | convolution fusion | flops 18923520 | bytes 1771008 | tf_op jit(solution)/shard_map/kpf,spf->ksf/dot_general | solution.py:45
  49.4 0.0 copy-done.3
  49.4 0.0 copy-done.4
  49.4 0.0 copy-done.5
  49.4 4.4 %add_bitcast_fusion.1 = f32[8,8,384]{0,1,2:T(8,128)} fusion(f32[384,8,8]{2,1,0:T(8,128)S(1)} %copy-done.4, f32[384,8,8]{2,1,0:T(8,128)S(1)} %copy-done.10, f32[8,64,384]{1,0,2:T(8,128)S(1)} %copy-done.5, f32[8,64,384]{1,0,2:T(8,128)S(1)} %copy-done.3, f32[384]{0:T(512)S(1)} %broadcast_subtract_fusion, f32[384]{0:T(512)S(1)} %fusion.38), kind=kOutput, calls=%fused_computation.6 | convolution fusion | flops 18972672 | bytes 1870848 | tf_op jit(solution)/shard_map/kpf,spf->ksf/dot_general | solution.py:48
  53.8 2.5 %copy.18 = f32[8,8,384]{2,1,0:T(8,128)} copy(f32[8,8,384]{0,1,2:T(8,128)} %add_bitcast_fusion.1) | data formatting | bytes 196608 | tf_op jit(solution)/shard_map/add | solution.py:51
  56.3 2.5 %copy.17 = f32[8,8,384]{2,1,0:T(8,128)} copy(f32[8,8,384]{0,1,2:T(8,128)} %subtract_bitcast_fusion.1) | data formatting | bytes 196608 | tf_op jit(solution)/shard_map/sub | solution.py:50
  58.8 2.3 broadcast_multiply_fusion.1
  61.0 0.8 copy-done.11
  61.8 2.6 %convolution_bitcast_fusion.2 = f32[1,64,384]{2,1,0:T(8,128)} fusion(f32[384,384]{1,0:T(8,128)} %get-tuple-element.17, f32[384,384]{1,0:T(8,128)S(1)} %broadcast_multiply_fusion.1, f32[8,8,384]{2,1,0:T(8,128)} %copy.18, f32[8,8,384]{2,1,0:T(8,128)} %copy.17), kind=kOutput, calls=%fused_computation.13 | convolution fusion | flops 227131392 | bytes 1474560 | tf_op jit(solution)/shard_map/ksf,ft->kst/dot_general | solution.py:76
  64.4 0.0 all-gather.2.cloned.1.call-update
  64.5 0.4 reduce-scatter.2.cloned.1.call-start
  64.9 2.8 %copy.19 = f32[8,64,384]{1,0,2:T(8,128)} copy(f32[8,64,384]{2,1,0:T(8,128)} %get-tuple-element.8) | data formatting | bytes 1572864 | tf_op jit(solution)/shard_map/slice | solution.py:44
  67.7 2.8 %copy.27 = f32[8,64,384]{1,0,2:T(8,128)} copy(f32[8,64,384]{2,1,0:T(8,128)} %get-tuple-element.7) | data formatting | bytes 1572864 | tf_op jit(solution)/shard_map/slice | solution.py:44
  70.5 0.0 copy-done.20
  70.5 0.2 convolution_bitcast_fusion.3
  70.7 1.5 fusion.28
  72.2 93.9 %all-gather.2.cloned.1.call-done = f32[32,64,384]{2,1,0:T(8,128)} async-done(((f32[1,64,384]{2,1,0:T(8,128)}), f32[32,64,384]{2,1,0:T(8,128)}) %all-gather.2.cloned.1.call-update) | async-done | bytes 3145744 | tf_op jit(solution)/shard_map/all_gather | solution.py:78
  166.1 2.7 %reduce_sum.20 = f32[64,384]{1,0:T(8,128)} reduce(f32[32,64,384]{2,1,0:T(8,128)} %all-gather.2.cloned.1.call-done, f32[]{:T(128)} %constant.85.clone.1), dimensions={0}, to_apply=%region_0.1 | reduce | flops 761856 | bytes 3244036 | tf_op jit(solution)/shard_map/reduce_sum | solution.py:78
  168.8 3.4 %fusion.24 = f32[64,4,384]{2,0,1:T(8,128)S(1)} fusion(f32[4,384,384]{2,1,0:T(8,128)S(1)} %copy-done, f32[64,384]{1,0:T(8,128)} %reduce_sum.20), kind=kOutput, calls=%fused_computation.43 | convolution fusion | flops 452984832 | bytes 2850816 | tf_op jit(solution)/shard_map/rt,but->rbu/dot_general | solution.py:64
  172.2 1.2 fusion.15
  173.4 0.8 fusion.5
  174.3 1.7 copy.29
  176.0 1.6 copy.28
  177.6 5.4 %fusion.53 = f32[384,64,8]{1,2,0:T(8,128)S(1)} fusion(f32[8,64,384]{1,0,2:T(8,128)} %copy.19, f32[8,8,384]{0,1,2:T(8,128)} %copy.29), kind=kOutput, calls=%fused_computation.88 | convolution fusion | flops 18874368 | bytes 1671168 | tf_op jit(solution)/shard_map/ksf,spf->kpf/dot_general | solution.py:46
  183.0 3.5 %fusion.54 = f32[384,64,8]{1,2,0:T(8,128)S(1)} fusion(f32[8,64,384]{1,0,2:T(8,128)S(1)} %copy-done.6, f32[8,8,384]{0,1,2:T(8,128)S(1)} %copy-done.9), kind=kOutput, calls=%fused_computation.89 | convolution fusion | flops 18874368 | bytes 1671168 | tf_op jit(solution)/shard_map/ksf,spf->kpf/dot_general | solution.py:47
  186.5 3.6 %subtract_bitcast_fusion = f32[8,64,384]{1,0,2:T(8,128)S(1)} fusion(f32[384,64,8]{1,2,0:T(8,128)S(1)} %fusion.53, f32[8,64,384]{1,0,2:T(8,128)S(1)} %copy-done.1, f32[8,8,384]{0,1,2:T(8,128)S(1)} %copy-done.9, f32[384]{0:T(512)S(1)} %fusion.38), kind=kOutput, calls=%fused_computation.5 | convolution fusion | flops 19267584 | bytes 2459136 | tf_op jit(solution)/shard_map/ksf,spf->kpf/dot_general | solution.py:45
  190.1 4.2 %add_bitcast_fusion = f32[8,64,384]{1,0,2:T(8,128)S(1)} fusion(f32[384,64,8]{1,2,0:T(8,128)S(1)} %fusion.53, f32[384,64,8]{1,2,0:T(8,128)S(1)} %fusion.54, f32[8,64,384]{1,0,2:T(8,128)S(1)} %copy-done.1, f32[8,8,384]{0,1,2:T(8,128)S(1)} %copy-done.2, f32[384]{0:T(512)S(1)} %broadcast_subtract_fusion, f32[384]{0:T(512)S(1)} %fusion.38), kind=kOutput, calls=%fused_computation.4 | convolution fusion | flops 19660800 | bytes 3247104 | tf_op jit(solution)/shard_map/ksf,spf->kpf/dot_general | solution.py:48
  194.3 0.2 pad_maximum_fusion
  194.5 0.8 copy-done.12
  195.4 0.2 copy-done.13
  195.6 6.6 %fusion = f32[8,64,384]{2,1,0:T(8,128)} fusion(f32[8,64,768]{1,0,2:T(8,128)S(1)} %pad_maximum_fusion, f32[384,384]{1,0:T(8,128)S(1)} %copy-done.13, f32[384,384]{1,0:T(8,128)S(1)} %copy-done.12), kind=kOutput, calls=%fused_computation.2 | convolution fusion | flops 1812529152 | bytes 3538944 | tf_op jit(solution)/shard_map/kpf,ft->kpt/dot_general | solution.py:89
  202.1 0.0 reduce-scatter.2.cloned.1.call-update
  202.2 0.8 constant_dynamic-slice_fusion.1
  202.9 3.1 %collective-permute-start = (f32[1,16,384]{2,1,0:T(8,128)S(1)}, f32[1,16,384]{2,1,0:T(8,128)S(1)}, u32[]{:S(2)}, u32[]{:S(2)}) collective-permute-start(f32[1,16,384]{2,1,0:T(8,128)S(1)} %get-tuple-element.13), channel_id=1, source_target_pairs={{0,1},{1,2},{2,3},{3,4},{4,5},{5,6},{6,7},{7,8},{8,9},{9,10},{10,1... | collective-permute-start | bytes 73736 | tf_op jit(solution)/shard_map/ppermute | solution.py:16
  206.0 2.7 %collective-permute-start.1 = (f32[1,16,384]{2,1,0:T(8,128)S(1)}, f32[1,16,384]{2,1,0:T(8,128)S(1)}, u32[]{:S(2)}, u32[]{:S(2)}) collective-permute-start(f32[1,16,384]{2,1,0:T(8,128)S(1)} %get-tuple-element.14), channel_id=1, source_target_pairs={{1,0},{2,1},{3,2},{4,3},{5,4},{6,5},{7,6},{8,7},{9,8},{10,9},{11,1... | collective-permute-start | bytes 73736 | tf_op jit(solution)/shard_map/ppermute | solution.py:19
  208.8 0.1 reshape.102
  208.9 0.9 constant_dynamic-slice_fusion.2
  209.8 0.9 fusion.75
  210.7 0.0 collective-permute-done
  210.7 1.0 collective-permute-done.1
  211.8 0.0 copy-start.17
  211.8 0.0 copy-start.19
  211.8 1.0 gather_fusion
  212.8 0.1 multiply_reduce_fusion
  212.9 22.7 %reduce-scatter.2.cloned.1.call-done = f32[1,64,384]{2,1,0:T(8,128)} async-done(((f32[8,64,384]{2,1,0:T(8,128)}), f32[1,64,384]{2,1,0:T(8,128)}) %reduce-scatter.2.cloned.1.call-update) | async-done | bytes 98320 | tf_op jit(solution)/shard_map/reduce_scatter | solution.py:88
  235.7 1.7 fusion.20
  (40 shorter events, 0.1 us)
Async XLA Ops:
  6.5 162.3 %copy-start = (f32[4,384,384]{2,1,0:T(8,128)S(1)}, f32[4,384,384]{2,1,0:T(8,128)}, u32[]{:S(2)}) copy-start(f32[4,384,384]{2,1,0:T(8,128)} %param.12) | copy-start | bytes 7077892
  6.5 159.6 %all-gather.2.cloned.1.call-start = ((), (), s32[]{:S(2)}) async-start(), calls=%async_computation.1 | async-start | bytes 3244032 | tf_op jit(solution)/shard_map/all_gather | solution.py:78
  6.5 5.6 %copy-start.15 = (f32[8,64,384]{2,1,0:T(8,128)S(1)}, f32[8,64,384]{2,1,0:T(8,128)}, u32[]{:S(2)}) copy-start(f32[8,64,384]{2,1,0:T(8,128)} %param.8) | copy-start | bytes 2359300
  30.2 5.9 %copy-start.7 = (f32[8,64,384]{1,0,2:T(8,128)S(1)}, f32[8,64,384]{1,0,2:T(8,128)}, u32[]{:S(2)}) copy-start(f32[8,64,384]{1,0,2:T(8,128)} %copy.15) | copy-start | bytes 2359300
  30.2 5.9 %copy-start.8 = (f32[8,64,384]{1,0,2:T(8,128)S(1)}, f32[8,64,384]{1,0,2:T(8,128)}, u32[]{:S(2)}) copy-start(f32[8,64,384]{1,0,2:T(8,128)} %copy.23) | copy-start | bytes 2359300
  43.0 6.4 %copy-start.3 = (f32[8,64,384]{1,0,2:T(8,128)S(1)}, f32[8,64,384]{1,0,2:T(8,128)}, u32[]{:S(2)}) copy-start(f32[8,64,384]{1,0,2:T(8,128)} %copy.16) | copy-start | bytes 2359300
  43.0 6.4 %copy-start.4 = (f32[384,8,8]{2,1,0:T(8,128)S(1)}, f32[384,8,8]{2,1,0:T(8,128)}, u32[]{:S(2)}) copy-start(f32[384,8,8]{2,1,0:T(8,128)} %fusion.51) | copy-start | bytes 294916
  43.0 6.4 %copy-start.5 = (f32[8,64,384]{1,0,2:T(8,128)S(1)}, f32[8,64,384]{1,0,2:T(8,128)}, u32[]{:S(2)}) copy-start(f32[8,64,384]{1,0,2:T(8,128)} %copy.22) | copy-start | bytes 2359300
  43.0 6.4 %copy-start.10 = (f32[384,8,8]{2,1,0:T(8,128)S(1)}, f32[384,8,8]{2,1,0:T(8,128)}, u32[]{:S(2)}) copy-start(f32[384,8,8]{2,1,0:T(8,128)} %fusion.52) | copy-start | bytes 294916
  61.0 0.8 copy-start.11
  64.5 171.2 %reduce-scatter.2.cloned.1.call-start = ((), (), s32[]{:S(2)}) async-start(), calls=%async_computation.2 | async-start | bytes 884736 | tf_op jit(solution)/shard_map/reduce_scatter | solution.py:88
  67.7 2.8 %copy-start.20 = (f32[8]{0:T(128)S(1)}, f32[8]{0:T(128)}, u32[]{:S(2)}) copy-start(f32[8]{0:T(128)} %param.10) | copy-start | bytes 100
  168.8 3.4 %copy-start.16 = (f32[64,4]{1,0:T(8,128)S(1)}, f32[64,4]{1,0:T(8,128)}, u32[]{:S(2)}) copy-start(f32[64,4]{1,0:T(8,128)} %fusion.28) | copy-start | bytes 3076
  168.8 4.6 %copy-start.14 = (f32[64,384]{1,0:T(8,128)S(1)}, f32[64,384]{1,0:T(8,128)}, u32[]{:S(2)}) copy-start(f32[64,384]{1,0:T(8,128)} %reduce_sum.20) | copy-start | bytes 294916
  177.6 5.4 %copy-start.6 = (f32[8,64,384]{1,0,2:T(8,128)S(1)}, f32[8,64,384]{1,0,2:T(8,128)}, u32[]{:S(2)}) copy-start(f32[8,64,384]{1,0,2:T(8,128)} %copy.19) | copy-start | bytes 2359300
  177.6 5.4 %copy-start.9 = (f32[8,8,384]{0,1,2:T(8,128)S(1)}, f32[8,8,384]{0,1,2:T(8,128)}, u32[]{:S(2)}) copy-start(f32[8,8,384]{0,1,2:T(8,128)} %copy.28) | copy-start | bytes 294916
  183.0 3.5 %copy-start.1 = (f32[8,64,384]{1,0,2:T(8,128)S(1)}, f32[8,64,384]{1,0,2:T(8,128)}, u32[]{:S(2)}) copy-start(f32[8,64,384]{1,0,2:T(8,128)} %copy.27) | copy-start | bytes 2359300
  186.5 3.6 %copy-start.2 = (f32[8,8,384]{0,1,2:T(8,128)S(1)}, f32[8,8,384]{0,1,2:T(8,128)}, u32[]{:S(2)}) copy-start(f32[8,8,384]{0,1,2:T(8,128)} %copy.29) | copy-start | bytes 294916
  194.3 1.1 copy-start.12
  194.3 1.2 copy-start.13
  195.5 13.2 %copy-start.18 = (s32[4,64]{1,0:T(4,128)S(1)}, s32[4,64]{1,0:T(4,128)}, u32[]{:S(2)}) copy-start(s32[4,64]{1,0:T(4,128)} %param.15) | copy-start | bytes 3076
  202.9 7.8 %collective-permute-start = (f32[1,16,384]{2,1,0:T(8,128)S(1)}, f32[1,16,384]{2,1,0:T(8,128)S(1)}, u32[]{:S(2)}, u32[]{:S(2)}) collective-permute-start(f32[1,16,384]{2,1,0:T(8,128)S(1)} %get-tuple-element.13), channel_id=1, source_target_pairs={{0,1},{1,2},{2,3},{3,4},{4,5},{5,6},{6,7},{7,8},{8,9},{9,10},{10,1... | collective-permute-start | bytes 73736 | tf_op jit(solution)/shard_map/ppermute | solution.py:16
  206.0 5.7 %collective-permute-start.1 = (f32[1,16,384]{2,1,0:T(8,128)S(1)}, f32[1,16,384]{2,1,0:T(8,128)S(1)}, u32[]{:S(2)}, u32[]{:S(2)}) collective-permute-start(f32[1,16,384]{2,1,0:T(8,128)S(1)} %get-tuple-element.14), channel_id=1, source_target_pairs={{1,0},{2,1},{3,2},{4,3},{5,4},{6,5},{7,6},{8,7},{9,8},{10,9},{11,1... | collective-permute-start | bytes 73736 | tf_op jit(solution)/shard_map/ppermute | solution.py:19
  211.8 1.0 copy-start.17
  211.8 23.9 %copy-start.19 = (f32[64]{0:T(128)S(1)}, f32[64]{0:T(128)}, u32[]{:S(2)}) copy-start(f32[64]{0:T(128)} %param.13) | copy-start | bytes 772
Sparse Core Ops, SparseCore 0:
  64.6 101.4 all-gather.1
  202.3 33.3 reduce-scatter.1
